TPU v7x, 128 devices: a whole 4x4x4 slice. The times are simulated.
128 devices in a mesh: chan: 16 (over z, x_hi, core), win: 8 (over y, x_lo).
Axes of the slice: x: 4 (x_hi: 2, x_lo: 2; x = x_hi * 2 + x_lo), y: 4, z: 4, core: 2. Of those that a mesh axis runs over, the one named last changes fastest.
Arguments:
- series: bfloat16 [64, 2048, 1500], P('win', 'chan'), may hold values from -1700 to 1700
- validity: int32 [64, 2048], P('win', 'chan'), may hold values from 0 to 1, as said below
Outputs:
- source_gathers: float32 [2048, 16, 8, 16, 128], P('chan', None, 'win')
Inputs may be any that keep to these rules, and one draw needn't show every extreme that they name: `validity`: a channel flagged dead is 0 in every window.
All inputs are finite; a program needn't handle non-finite values.
Results may differ from a plain program's by a relative error of at most 0.0037.
Values may be sent and summed in bfloat16 or wider, within the bound.
No kernel may reach another device: no remote copies, remote signals or barrier semaphores. Data moves between devices by JAX's collectives and lax.ppermute only.
A program may use at most 192 MiB of HBM per device.

v0:
```python
import math
import jax
import jax.numpy as jnp
from jax import lax
from jax.sharding import PartitionSpec as P

CHANNELS = 2048
SAMPLES = 1500
BINS = 128
LAGS = 128
SOURCES = 2048
lowest_bin = 6


def build_tables():
    sample_idx = jnp.arange(SAMPLES, dtype=jnp.int32)
    bin_idx = jnp.arange(BINS, dtype=jnp.int32) + lowest_bin
    phase_index = sample_idx[:, None] * bin_idx[None, :] % SAMPLES
    phase_angle = phase_index.astype(jnp.float32) * (2.0 * math.pi / SAMPLES)
    hann_taper = 0.5 - 0.5 * jnp.cos(sample_idx.astype(jnp.float32) * (2.0 * math.pi / SAMPLES))
    taper_table = jnp.concatenate(
        [hann_taper[:, None] * jnp.cos(phase_angle), -hann_taper[:, None] * jnp.sin(phase_angle)],
        axis=1,
    ).astype(jnp.bfloat16)
    lag_idx = jnp.arange(LAGS, dtype=jnp.int32) - LAGS // 2
    lag_index = bin_idx[:, None] * lag_idx[None, :] % SAMPLES
    lag_angle = lag_index.astype(jnp.float32) * (2.0 * math.pi / SAMPLES)
    inverse = jnp.concatenate([jnp.cos(lag_angle), -jnp.sin(lag_angle)], axis=0)
    return (taper_table, inverse)


def pair_block(src_spec, src_flags, recv_spec, recv_flags, inverse):
    src_real = src_spec[..., :BINS]
    src_imag = src_spec[..., BINS:]
    recv_real = recv_spec[..., :BINS]
    recv_imag = recv_spec[..., BINS:]
    in_phase = jnp.einsum("wsk,wik->sik", src_real, recv_real, preferred_element_type=jnp.float32)
    in_phase = in_phase + jnp.einsum(
        "wsk,wik->sik", src_imag, recv_imag, preferred_element_type=jnp.float32
    )
    quadrature = jnp.einsum("wsk,wik->sik", src_real, recv_imag, preferred_element_type=jnp.float32)
    quadrature = quadrature - jnp.einsum(
        "wsk,wik->sik", src_imag, recv_real, preferred_element_type=jnp.float32
    )
    joined = jnp.concatenate([in_phase, quadrature], axis=-1)
    lead_rows, recv_rows, spec_width = joined.shape
    lagged = jnp.dot(
        joined.reshape(lead_rows * recv_rows, spec_width),
        inverse,
        precision=lax.Precision.HIGHEST,
        preferred_element_type=jnp.float32,
    )
    lagged = lagged.reshape(lead_rows, recv_rows, LAGS)
    pair_count = jnp.einsum("ws,wi->si", src_flags, recv_flags, preferred_element_type=jnp.float32)
    return (lagged, pair_count)


def on_device(series, validity):
    win_rows, channel_count, samples = series.shape
    taper_table, inverse = build_tables()
    spectra = jnp.dot(
        series.reshape(win_rows * channel_count, samples),
        taper_table,
        preferred_element_type=jnp.float32,
    )
    spectra = spectra.reshape(win_rows, channel_count, 2 * BINS)
    energy = jnp.mean(spectra * spectra, axis=-1, keepdims=True)
    flag_float = validity.astype(jnp.float32)
    whitened = (spectra * lax.rsqrt(energy + 1e-06) * flag_float[..., None]).astype(jnp.bfloat16)
    flag_half = validity.astype(jnp.bfloat16)
    stride = CHANNELS // SOURCES
    src_spec, src_flags = (
        lax.all_gather(whitened, "win", axis=0, tiled=True),
        lax.all_gather(flag_half, "win", axis=0, tiled=True),
    )
    blocks = lax.axis_size("chan")
    slot_count = lax.axis_size("win")
    slot_width = channel_count // slot_count
    own_sources = src_spec.shape[1]
    every_spec, every_flags = (
        lax.all_gather(whitened, "chan", axis=1, tiled=True),
        lax.all_gather(flag_half, "chan", axis=1, tiled=True),
    )
    every_spec = every_spec.reshape(win_rows, blocks, slot_count, slot_width, 2 * BINS)
    every_flags = every_flags.reshape(win_rows, blocks, slot_count, slot_width)
    recv_spec, recv_flags = (
        lax.all_to_all(every_spec, "win", split_axis=2, concat_axis=0, tiled=True),
        lax.all_to_all(every_flags, "win", split_axis=2, concat_axis=0, tiled=True),
    )
    recv_spec = recv_spec.reshape(win_rows * slot_count, blocks * slot_width, 2 * BINS)
    recv_flags = recv_flags.reshape(win_rows * slot_count, blocks * slot_width)
    stacked, pair_count = pair_block(src_spec, src_flags, recv_spec, recv_flags, inverse)
    result = stacked / jnp.maximum(pair_count, 1.0)[..., None]
    return result.reshape(own_sources, blocks, 1, slot_width, LAGS)


def solution(mesh):
    return jax.shard_map(
        on_device,
        mesh=mesh,
        in_specs=(P("win", "chan", None), P("win", "chan")),
        out_specs=P("chan", None, "win", None, None),
        check_vma=False,
    )
```

profile of v0, /device:TPU:0, one launch (start us, length us, event | category | flops | bytes accessed | tf_op | source)
XLA Modules:
  0.0 466.3 jit_solution(18213554256155514033)
XLA Ops:
  6.6 2.0 pad.6
  8.6 0.8 copy.22
  9.4 3.4 multiply_convert_fusion.2
  12.8 1.0 multiply_reduce_fusion
  13.8 0.3 copy.17
  14.2 1.2 multiply_convert_fusion
  15.5 0.7 all-gather.5.cloned.1.call-update
  16.2 25.9 %all_gather.15 = bf16[8,2048]{1,0:T(8,128)(2,1)S(1)} all-gather(bf16[8,128]{1,0:T(8,128)(2,1)S(1)} %get-tuple-element.10), channel_id=1, replica_groups=mesh['chan'=16,'win'=8] {'chan'}, dimensions={1}, use_global_device_ids=true | all-gather | bytes 34816 | tf_op jit(solution)/shard_map/all_gather | solution.py:82
  42.0 0.2 reshape.74
  42.3 0.9 reshape.78
  43.2 4.5 all-to-all-start.1
  47.7 43.3 %all-gather.3.cloned.1.call-done = bf16[8,2048,256]{2,1,0:T(8,128)(2,1)} async-done(((bf16[8,128,256]{2,1,0:T(8,128)(2,1)}), bf16[8,2048,256]{2,1,0:T(8,128)(2,1)}) %all-gather.3.cloned.1.call-update) | async-done | bytes 8388624 | tf_op jit(solution)/shard_map/all_gather | solution.py:81
  91.0 8.0 %copy.9 = bf16[8,16,8,16,256]{4,3,1,0,2:T(8,128)(2,1)} copy(bf16[8,16,8,16,256]{4,3,2,1,0:T(8,128)(2,1)} %bitcast.52) | data formatting | bytes 16777216 | tf_op jit(solution)/shard_map/reshape | solution.py:84
  99.0 5.0 %all-to-all-start = ((bf16[8,16,8,16,256]{4,3,1,0,2:T(8,128)(2,1)}), bf16[8,16,8,16,256]{4,3,1,0,2:T(8,128)(2,1)}, u32[]{:S(2)}, u32[]{:S(2)}) async-start(bf16[8,16,8,16,256]{4,3,1,0,2:T(8,128)(2,1)} %copy.9), calls=%async_computation | async-start | bytes 16777216 | tf_op jit(solution)/shard_map/all_to_all | solution.py:87
  104.0 186.0 %all_gather.14 = bf16[64,128]{1,0:T(8,128)(2,1)S(1)} all-gather(bf16[8,128]{1,0:T(8,128)(2,1)S(1)} %get-tuple-element.10), channel_id=1, replica_groups=mesh['chan'=16,'win'=8] {'win'}, dimensions={0}, use_global_device_ids=true | all-gather | bytes 18432 | tf_op jit(solution)/shard_map/all_gather | solution.py:74
  290.0 0.3 fusion.14
  290.3 0.2 reshape.79
  290.6 0.2 reshape.75
  290.8 0.2 convolution_maximum_fusion
  291.1 4.0 fusion.20
  295.0 2.9 copy.19
  297.9 3.3 copy.21
  301.2 6.1 %fusion.19 = (bf16[64,256,128]{2,1,0:T(8,128)(2,1)}, bf16[64,256,128]{2,1,0:T(8,128)(2,1)}) fusion(bf16[64,256,256]{2,1,0:T(8,128)(2,1)} %bitcast.6), kind=kLoop, calls=%fused_computation.39 | loop fusion | bytes 16777216 | tf_op jit(solution)/shard_map/slice | solution.py:35
  307.3 6.9 %copy.18 = bf16[64,256,128]{1,0,2:T(8,128)(2,1)} copy(bf16[64,256,128]{2,1,0:T(8,128)(2,1)} %get-tuple-element.5) | data formatting | bytes 8388608
  314.2 6.8 %copy.20 = bf16[64,256,128]{1,0,2:T(8,128)(2,1)} copy(bf16[64,256,128]{2,1,0:T(8,128)(2,1)} %get-tuple-element.6) | data formatting | bytes 8388608
  321.0 11.1 %fusion.22 = f32[128,256,128]{2,1,0:T(8,128)} fusion(bf16[64,256,128]{1,0,2:T(8,128)(2,1)} %copy.18, bf16[64,128,128]{1,0,2:T(8,128)(2,1)} %copy.19), kind=kOutput, calls=%fused_computation.44 | convolution fusion | flops 536870912 | bytes 23068672 | tf_op jit(solution)/shard_map/wsk,wik->sik/dot_general | solution.py:37
  332.1 7.5 %fusion.23 = f32[128,256,128]{2,1,0:T(8,128)} fusion(bf16[64,256,128]{1,0,2:T(8,128)(2,1)S(1)} %copy-done, bf16[64,128,128]{1,0,2:T(8,128)(2,1)S(1)} %copy-done.1), kind=kOutput, calls=%fused_computation.45 | convolution fusion | flops 536870912 | bytes 23068672 | tf_op jit(solution)/shard_map/wsk,wik->sik/dot_general | solution.py:41
  339.6 15.2 %add_bitcast_fusion = f32[128,256,128]{0,1,2:T(8,128)} fusion(f32[128,256,128]{2,1,0:T(8,128)} %fusion.22, bf16[64,256,128]{1,0,2:T(8,128)(2,1)} %copy.20, bf16[64,128,128]{1,0,2:T(8,128)(2,1)S(1)} %copy.21), kind=kOutput, calls=%fused_computation.2 | convolution fusion | flops 541065216 | bytes 39845888 | tf_op jit(solution)/shard_map/wsk,wik->sik/dot_general | solution.py:38
  354.7 15.6 %subtract_bitcast_fusion = f32[128,256,128]{0,1,2:T(8,128)} fusion(f32[128,256,128]{2,1,0:T(8,128)} %fusion.23, bf16[64,256,128]{1,0,2:T(8,128)(2,1)} %copy.18, bf16[64,128,128]{1,0,2:T(8,128)(2,1)S(1)} %copy.21), kind=kOutput, calls=%fused_computation.1 | convolution fusion | flops 541065216 | bytes 39845888 | tf_op jit(solution)/shard_map/wsk,wik->sik/dot_general | solution.py:42
  370.3 23.2 %pad_maximum_fusion = f32[128,256,256]{0,1,2:T(8,128)} fusion(f32[128,256,128]{0,1,2:T(8,128)} %subtract_bitcast_fusion, f32[128,256,128]{0,1,2:T(8,128)} %add_bitcast_fusion), kind=kLoop, calls=%fused_computation | loop fusion | flops 8388608 | bytes 67108864 | tf_op jit(solution)/shard_map/concatenate | solution.py:45
  393.5 33.6 %copy.14 = f32[128,256,256]{2,1,0:T(8,128)} copy(f32[128,256,256]{0,1,2:T(8,128)} %pad_maximum_fusion) | data formatting | bytes 67108864 | tf_op jit(solution)/shard_map/concatenate | solution.py:45
  427.1 32.4 %broadcast_divide_fusion = f32[128,256,128]{2,1,0:T(8,128)} fusion(f32[128,256]{1,0:T(8,128)S(1)} %convolution_maximum_fusion, f32[128,256,256]{2,1,0:T(8,128)} %copy.14, f32[128,128]{1,0:T(8,128)S(1)} %get-tuple-element.12, f32[128,128]{1,0:T(8,128)S(1)} %get-tuple-element.11), kind=kOutput, calls=%fused_computation.3 | convolution fusion | flops 12889128960 | bytes 50593792 | tf_op jit(solution)/shard_map/dot_general | solution.py:47
  (18 shorter events, 0.2 us)
Async XLA Ops:
  6.5 84.4 %all-gather.3.cloned.1.call-start = ((), (), s32[]{:S(2)}) async-start(), calls=%async_computation.2 | async-start | bytes 8912896 | tf_op jit(solution)/shard_map/all_gather | solution.py:81
  12.8 1.4 copy-start.2
  15.4 275.6 %all-gather.5.cloned.1.call-start = ((), (), s32[]{:S(2)}) async-start(), calls=%async_computation.3 | async-start | bytes 4718592 | tf_op jit(solution)/shard_map/all_gather | solution.py:73
  43.2 55.8 %all-to-all-start.1 = ((bf16[8,2,1024]{2,1,0:T(2,128)(2,1)}), bf16[8,2,1024]{2,1,0:T(2,128)(2,1)S(1)}, u32[]{:S(2)}, u32[]{:S(2)}) async-start(bf16[8,2,1024]{2,1,0:T(2,128)(2,1)} %reshape.78), calls=%async_computation.1 | async-start | bytes 65536 | tf_op jit(solution)/shard_map/all_to_all | solution.py:88
  99.0 202.2 %all-to-all-start = ((bf16[8,16,8,16,256]{4,3,1,0,2:T(8,128)(2,1)}), bf16[8,16,8,16,256]{4,3,1,0,2:T(8,128)(2,1)}, u32[]{:S(2)}, u32[]{:S(2)}) async-start(bf16[8,16,8,16,256]{4,3,1,0,2:T(8,128)(2,1)} %copy.9), calls=%async_computation | async-start | bytes 16777216 | tf_op jit(solution)/shard_map/all_to_all | solution.py:87
  321.0 11.1 %copy-start = (bf16[64,256,128]{1,0,2:T(8,128)(2,1)S(1)}, bf16[64,256,128]{1,0,2:T(8,128)(2,1)}, u32[]{:S(2)}) copy-start(bf16[64,256,128]{1,0,2:T(8,128)(2,1)} %copy.20) | copy-start | bytes 12582916
  321.0 11.1 %copy-start.1 = (bf16[64,128,128]{1,0,2:T(8,128)(2,1)S(1)}, bf16[64,128,128]{1,0,2:T(8,128)(2,1)}, u32[]{:S(2)}) copy-start(bf16[64,128,128]{1,0,2:T(8,128)(2,1)} %copy.19) | copy-start | bytes 6291460
Sparse Core Ops, SparseCore 0:
  15.5 75.3 all-gather.2
  92.6 159.8 all-gather.4
where the time goes:
time: 467 us; the launch traced here: 466 us
  blocking collectives  212 us (45%)
  matrix products  82.9 us (18%)
  local copies, waits for them, and re-layouts  76.3 us (16%)
  waiting for transfers between devices  44 us (9%)
  other arithmetic  28.1 us (6%)
  between operations  13.6 us (3%)
  starting transfers between devices  9.5 us (2%)
    all_gather x1, blocking collectives, on_device(): lax.all_gather(flag_half, 'win', axis=0, tiled=True)  186 us
    all_gather x1, waiting for transfers between devices, on_device(): lax.all_gather(whitened, 'chan', axis=1, tiled=True)  43.3 us
    concatenate x1, local copies, waits for them, and re-layouts, pair_block(): joined = jnp.concatenate([in_phase, quadrature], axis=-1)  33.6 us
    dot_general x1, matrix products, pair_block(): jnp.dot(joined.reshape(lead_rows * recv_rows, spec_width), inverse, preci...  32.4 us
    all_gather x1, blocking collectives, on_device(): lax.all_gather(flag_half, 'chan', axis=1, tiled=True)  25.9 us
    unnamed x14, local copies, waits for them, and re-layouts  23.8 us
    concatenate x1, other arithmetic, pair_block(): joined = jnp.concatenate([in_phase, quadrature], axis=-1)  23.2 us
    dot_general x1, matrix products, pair_block(): jnp.einsum('wsk,wik->sik', src_imag, recv_real, preferred_element_type=jn...  15.6 us
  transfers between devices with their start and end apart: 4, of which 1 were waited for; matrix products, arithmetic and copies ran while one was open for 4% of the time, Pallas kernels for 0%

commit v1 on v0

--- a/solution.py
+++ b/solution.py
@@ -3,6 +3,7 @@
 import jax.numpy as jnp
 from jax import lax
 from jax.sharding import PartitionSpec as P
+from jax.lax import all_to_all, axis_size
 
 CHANNELS = 2048
 SAMPLES = 1500
@@ -56,6 +57,13 @@
 
 
 def on_device(series, validity):
+
+    def connect_side(x_local, named_axis, on_dim):
+        v_next = jnp.stack(axis_size(named_axis) * [x_local])
+        n_now = all_to_all(v_next, named_axis, 0, 0)
+        piece_out = jnp.concatenate(n_now, axis=on_dim)
+        return piece_out
+
     win_rows, channel_count, samples = series.shape
     taper_table, inverse = build_tables()
     spectra = jnp.dot(
@@ -78,7 +86,7 @@
     slot_width = channel_count // slot_count
     own_sources = src_spec.shape[1]
     every_spec, every_flags = (
-        lax.all_gather(whitened, "chan", axis=1, tiled=True),
+        connect_side(whitened, named_axis="chan", on_dim=1),
         lax.all_gather(flag_half, "chan", axis=1, tiled=True),
     )
     every_spec = every_spec.reshape(win_rows, blocks, slot_count, slot_width, 2 * BINS)

time: 467 us -> 516 us (1.10)
  blocking collectives: 212 us -> 300 us
  waiting for transfers between devices: 44 us -> 0.69 us
  starting transfers between devices: 9.5 us -> 18.3 us
  local copies, waits for them, and re-layouts: 76.3 us -> 70.7 us
    all_gather x1, blocking collectives: 25.9 us -> 110 us  [on_device(): lax.all_gather(flag_half, 'chan', axis=1, tiled=True)]
    all_gather x1 -> x0, waiting for transfers between devices: 43.3 us -> none  [on_device(): lax.all_gather(whitened, 'chan', axis=1, tiled=True)]
    another operation x0 -> x2, local copies, waits for them, and re-layouts: none -> 12.5 us  [the longest x1 8.01 us: on_device(): every_spec.reshape(win_rows, blocks, slot_count, slot_width, 2 * BINS)]
    reshape x2 -> x0, local copies, waits for them, and re-layouts: 8.34 us -> none  [the longest x1 8.01 us: on_device(): every_spec.reshape(win_rows, blocks, slot_count, slot_width, 2 * BINS)]
    all_to_all x0 -> x1, starting transfers between devices: none -> 8.04 us  [connect_side(): n_now = all_to_all(v_next, named_axis, 0, 0)]
    unnamed x14 -> x15, local copies, waits for them, and re-layouts: 23.8 us -> 17.8 us
  transfers between devices with their start and end apart: 4 -> 4, of which waited for: 1 -> 0; matrix products, arithmetic and copies ran while one was open for 4% -> 6% of each run, Pallas kernels for 0% -> 0%
where the time goes in v1:
time: 516 us; the launch traced here: 515 us
  blocking collectives  300 us (58%)
  matrix products  84 us (16%)
  local copies, waits for them, and re-layouts  70.7 us (14%)
  other arithmetic  27.2 us (5%)
  starting transfers between devices  18.3 us (4%)
  between operations  13.6 us (3%)
    all_gather x1, blocking collectives, on_device(): lax.all_gather(flag_half, 'win', axis=0, tiled=True)  191 us
    all_gather x1, blocking collectives, on_device(): lax.all_gather(flag_half, 'chan', axis=1, tiled=True)  110 us
    concatenate x1, local copies, waits for them, and re-layouts, pair_block(): joined = jnp.concatenate([in_phase, quadrature], axis=-1)  33.6 us
    dot_general x1, matrix products, pair_block(): jnp.dot(joined.reshape(lead_rows * recv_rows, spec_width), inverse, preci...  32.4 us
    concatenate x1, other arithmetic, pair_block(): joined = jnp.concatenate([in_phase, quadrature], axis=-1)  23.3 us
    unnamed x15, local copies, waits for them, and re-layouts  17.8 us
    dot_general x1, matrix products, pair_block(): jnp.einsum('wsk,wik->sik', src_imag, recv_real, preferred_element_type=jn...  16.2 us
    dot_general x1, matrix products, pair_block(): jnp.einsum('wsk,wik->sik', src_imag, recv_imag, preferred_element_type=jn...  15.7 us
  transfers between devices with their start and end apart: 4, of which 0 were waited for; matrix products, arithmetic and copies ran while one was open for 6% of the time, Pallas kernels for 0%

profile of v1, /device:TPU:0, one launch (start us, length us, event | category | flops | bytes accessed | tf_op | source)
XLA Modules:
  0.0 514.8 jit_solution(16679361346861991136)
XLA Ops:
  6.5 0.1 multiply_subtract_fusion
  6.6 2.0 pad.6
  8.6 0.8 copy.26
  9.4 3.4 multiply_convert_fusion.1
  12.8 1.0 fusion.8
  13.8 0.2 copy.27
  14.1 0.1 fusion.7
  14.2 0.3 copy.15
  14.6 4.4 stack.2
  19.0 8.0 %all-to-all-start = ((bf16[16,8,128,256]{3,2,1,0:T(8,128)(2,1)}), bf16[16,8,128,256]{3,2,1,0:T(8,128)(2,1)}, u32[]{:S(2)}, u32[]{:S(2)}) async-start(bf16[16,8,128,256]{3,2,1,0:T(8,128)(2,1)} %stack.2), calls=%async_computation | async-start | bytes 16777216 | tf_op jit(solution)/shard_map/all_to_all | solution.py:63
  27.1 109.6 %all_gather.11 = bf16[8,2048]{1,0:T(8,128)(2,1)S(1)} all-gather(bf16[8,128]{1,0:T(8,128)(2,1)S(1)} %get-tuple-element.8), channel_id=1, replica_groups=mesh['chan'=16,'win'=8] {'chan'}, dimensions={1}, use_global_device_ids=true | all-gather | bytes 34816 | tf_op jit(solution)/shard_map/all_gather | solution.py:90
  136.6 0.2 reshape.77
  136.9 0.9 reshape.81
  137.8 4.5 all-to-all-start.2
  142.3 8.0 %copy.17 = bf16[8,16,8,16,256]{4,3,1,0,2:T(8,128)(2,1)} copy(bf16[8,16,8,16,256]{4,3,2,0,1:T(8,128)(2,1)} %bitcast.4) | data formatting | bytes 16777216 | tf_op jit(solution)/shard_map/reshape;reshape | solution.py:92
  150.3 5.7 %all-to-all-start.1 = ((bf16[8,16,8,16,256]{4,3,1,0,2:T(8,128)(2,1)}), bf16[8,16,8,16,256]{4,3,1,0,2:T(8,128)(2,1)}, u32[]{:S(2)}, u32[]{:S(2)}) async-start(bf16[8,16,8,16,256]{4,3,1,0,2:T(8,128)(2,1)} %copy.17), calls=%async_computation.1 | async-start | bytes 16777216 | tf_op jit(solution)/shard_map/all_to_all | solution.py:95
  156.0 0.7 all-gather.2.cloned.1.call-update
  156.7 190.7 %all_gather.10 = bf16[64,128]{1,0:T(8,128)(2,1)S(1)} all-gather(bf16[8,128]{1,0:T(8,128)(2,1)S(1)} %get-tuple-element.8), channel_id=1, replica_groups=mesh['chan'=16,'win'=8] {'win'}, dimensions={0}, use_global_device_ids=true | all-gather | bytes 18432 | tf_op jit(solution)/shard_map/all_gather | solution.py:82
  347.4 0.3 fusion.24
  347.8 0.2 reshape.82
  348.0 0.2 reshape.78
  348.3 0.2 convolution_maximum_fusion
  348.5 6.0 %fusion.29 = (bf16[64,256,128]{2,1,0:T(8,128)(2,1)}, bf16[64,256,128]{2,1,0:T(8,128)(2,1)}) fusion(bf16[64,256,256]{2,1,0:T(8,128)(2,1)} %bitcast.7), kind=kLoop, calls=%fused_computation.48 | loop fusion | bytes 16777216 | tf_op jit(solution)/shard_map/slice | solution.py:36
  354.5 6.8 %copy.24 = bf16[64,256,128]{1,0,2:T(8,128)(2,1)} copy(bf16[64,256,128]{2,1,0:T(8,128)(2,1)} %get-tuple-element.5) | data formatting | bytes 8388608
  361.3 6.9 %copy.25 = bf16[64,256,128]{1,0,2:T(8,128)(2,1)} copy(bf16[64,256,128]{2,1,0:T(8,128)(2,1)} %get-tuple-element.6) | data formatting | bytes 8388608
  368.2 11.1 %fusion.4 = f32[128,256,128]{2,1,0:T(8,128)} fusion(bf16[64,256,128]{1,0,2:T(8,128)(2,1)} %copy.24, bf16[64,128,256]{1,0,2:T(8,128)(2,1)} %all-gather.2.cloned.1.call-done), kind=kOutput, calls=%fused_computation.8 | convolution fusion | flops 536870912 | bytes 23068672 | tf_op jit(solution)/shard_map/wsk,wik->sik/dot_general | solution.py:38
  379.3 7.5 %fusion.2 = f32[128,256,128]{2,1,0:T(8,128)} fusion(bf16[64,256,128]{1,0,2:T(8,128)(2,1)S(1)} %copy-done, bf16[64,128,256]{1,0,2:T(8,128)(2,1)S(1)} %copy-done.1), kind=kOutput, calls=%fused_computation.6 | convolution fusion | flops 536870912 | bytes 23068672 | tf_op jit(solution)/shard_map/wsk,wik->sik/dot_general | solution.py:42
  386.7 15.7 %add_bitcast_fusion = f32[128,256,128]{0,1,2:T(8,128)} fusion(f32[128,256,128]{2,1,0:T(8,128)} %fusion.4, bf16[64,256,128]{1,0,2:T(8,128)(2,1)} %copy.25, bf16[64,128,256]{1,0,2:T(8,128)(2,1)} %all-gather.2.cloned.1.call-done), kind=kOutput, calls=%fused_computation.2 | convolution fusion | flops 541065216 | bytes 39845888 | tf_op jit(solution)/shard_map/wsk,wik->sik/dot_general | solution.py:39
  402.5 16.2 %subtract_bitcast_fusion = f32[128,256,128]{0,1,2:T(8,128)} fusion(f32[128,256,128]{2,1,0:T(8,128)} %fusion.2, bf16[64,256,128]{1,0,2:T(8,128)(2,1)} %copy.24, bf16[64,128,256]{1,0,2:T(8,128)(2,1)} %all-gather.2.cloned.1.call-done), kind=kOutput, calls=%fused_computation.1 | convolution fusion | flops 541065216 | bytes 39845888 | tf_op jit(solution)/shard_map/wsk,wik->sik/dot_general | solution.py:43
  418.6 23.3 %pad_maximum_fusion = f32[128,256,256]{0,1,2:T(8,128)} fusion(f32[128,256,128]{0,1,2:T(8,128)} %subtract_bitcast_fusion, f32[128,256,128]{0,1,2:T(8,128)} %add_bitcast_fusion), kind=kLoop, calls=%fused_computation | loop fusion | flops 8388608 | bytes 67108864 | tf_op jit(solution)/shard_map/concatenate | solution.py:46
  441.9 33.6 %copy.20 = f32[128,256,256]{2,1,0:T(8,128)} copy(f32[128,256,256]{0,1,2:T(8,128)} %pad_maximum_fusion) | data formatting | bytes 67108864 | tf_op jit(solution)/shard_map/concatenate | solution.py:46
  475.5 32.4 %broadcast_divide_fusion = f32[128,256,128]{2,1,0:T(8,128)} fusion(f32[128,256]{1,0:T(8,128)S(1)} %convolution_maximum_fusion, f32[128,256,256]{2,1,0:T(8,128)} %copy.20, f32[128,128]{1,0:T(8,128)S(1)} %get-tuple-element.10, f32[128,128]{1,0:T(8,128)S(1)} %get-tuple-element.9), kind=kOutput, calls=%fused_computation.3 | convolution fusion | flops 12889128960 | bytes 50593792 | tf_op jit(solution)/shard_map/dot_general | solution.py:48
  (18 shorter events, 0.1 us)
Async XLA Ops:
  12.8 1.3 copy-start.3
  14.2 4.8 copy-start.2
  19.0 118.8 %all-to-all-start = ((bf16[16,8,128,256]{3,2,1,0:T(8,128)(2,1)}), bf16[16,8,128,256]{3,2,1,0:T(8,128)(2,1)}, u32[]{:S(2)}, u32[]{:S(2)}) async-start(bf16[16,8,128,256]{3,2,1,0:T(8,128)(2,1)} %stack.2), calls=%async_computation | async-start | bytes 16777216 | tf_op jit(solution)/shard_map/all_to_all | solution.py:63
  137.8 12.5 %all-to-all-start.2 = ((bf16[8,2,1024]{2,1,0:T(2,128)(2,1)}), bf16[8,2,1024]{2,1,0:T(2,128)(2,1)S(1)}, u32[]{:S(2)}, u32[]{:S(2)}) async-start(bf16[8,2,1024]{2,1,0:T(2,128)(2,1)} %reshape.81), calls=%async_computation.2 | async-start | bytes 65536 | tf_op jit(solution)/shard_map/all_to_all | solution.py:96
  150.3 198.2 %all-to-all-start.1 = ((bf16[8,16,8,16,256]{4,3,1,0,2:T(8,128)(2,1)}), bf16[8,16,8,16,256]{4,3,1,0,2:T(8,128)(2,1)}, u32[]{:S(2)}, u32[]{:S(2)}) async-start(bf16[8,16,8,16,256]{4,3,1,0,2:T(8,128)(2,1)} %copy.17), calls=%async_computation.1 | async-start | bytes 16777216 | tf_op jit(solution)/shard_map/all_to_all | solution.py:95
  156.0 212.2 %all-gather.2.cloned.1.call-start = ((), (), s32[]{:S(2)}) async-start(), calls=%async_computation.3 | async-start | bytes 4718592 | tf_op jit(solution)/shard_map/all_gather | solution.py:81
  368.2 11.1 %copy-start = (bf16[64,256,128]{1,0,2:T(8,128)(2,1)S(1)}, bf16[64,256,128]{1,0,2:T(8,128)(2,1)}, u32[]{:S(2)}) copy-start(bf16[64,256,128]{1,0,2:T(8,128)(2,1)} %copy.25) | copy-start | bytes 12582916
  368.2 11.1 %copy-start.1 = (bf16[64,128,256]{1,0,2:T(8,128)(2,1)S(1)}, bf16[64,128,256]{1,0,2:T(8,128)(2,1)}, u32[]{:S(2)}) copy-start(bf16[64,128,256]{1,0,2:T(8,128)(2,1)} %all-gather.2.cloned.1.call-done) | copy-start | bytes 12582916
Sparse Core Ops, SparseCore 0:
  158.4 166.8 all-gather.1
